TPU v7x, 32 devices: a whole 2x2x4 slice. The times are simulated.
32 devices in a mesh: groups: 2 (over y), freq: 4 (over z), sub: 4 (over x, core).
Axes of the slice: x: 2, y: 2, z: 4, core: 2. Of those that a mesh axis runs over, the one named last changes fastest.
Arguments:
- wavenumbers: float32 [512, 300], replicated, may hold values from 1 to 20
- receiver_shapes: bfloat16 [512, 300], replicated, may hold values from -6 to 6
- source_shapes: bfloat16 [512, 4, 300], replicated, may hold values from -6 to 6
- mode_counts: int32 [512], replicated, may hold values from 64 to 300, as said below
- source_depths: int32 [32], P('groups'), parts along dimension 0, may hold values from 0 to 3
- source_ranges: float32 [32], P('groups'), parts along dimension 0, may hold values from 0 to 0.5
- sections: int32 [2048], P(('freq', 'sub')), may hold values from 0 to 511, as said below
- recorded: bfloat16 [2048, 4096], P(('freq', 'sub')), may hold values from -6 to 6
Outputs:
- scores: float32 [32, 512], P('groups', ('freq', 'sub')), parts along dimension 0
There are 2 independent parts, one for each index of `groups`. A program takes and returns all parts, laid end to end along the dimension named above; an argument that names none is the same for every part. Nothing has to cross between parts.
Inputs may be any that keep to these rules, and one draw needn't show every extreme that they name: `mode_counts`: counts rise with the bin index: bin f holds within 16 of 64 + floor((236) f / 511) modes, clipped to the range; the first bin holds 64 and the last 300. `sections`: each section holds exactly 4 channels.
All inputs are finite; a program needn't handle non-finite values.
Results may differ from a plain program's by a relative error of at most 0.0068.
Values may be sent and summed in bfloat16 or wider, within the bound.
A program may use at most 64 MiB of HBM per device.

v0:
```python
import math

import jax
import jax.numpy as jnp
from jax import lax
from jax.sharding import PartitionSpec as P

F = 512
NT = 4096
R = 2048
SEC = 512
F0 = 256


def source_factor(wave_part, source_table, counts, depths, ranges):
    depth_grid = source_table.shape[1]
    mode_width = wave_part.shape[1]
    chooser = (depths[:, None] == jnp.arange(depth_grid, dtype=jnp.int32)[None, :]).astype(
        jnp.float32
    )
    at_source = jnp.einsum(
        "sz,bzm->bsm", chooser, source_table.astype(jnp.float32), precision=lax.Precision.HIGHEST
    )
    mode_live = (jnp.arange(mode_width, dtype=jnp.int32)[None, :] < counts[:, None]).astype(
        jnp.float32
    )
    phases = wave_part[:, None, :] * ranges[None, :, None]
    weighted = at_source * mode_live[:, None, :]
    return jnp.concatenate(
        [weighted * jnp.cos(phases), -weighted * jnp.sin(phases)], axis=2
    ).astype(jnp.bfloat16)


def receiver_factor(wave_part, receiver_table, positions):
    mode_width = wave_part.shape[1]
    phases = wave_part[:, :, None] * positions[None, None, :]
    amplitude = receiver_table.astype(jnp.float32)[:, :, None] * 8.0 / jnp.sqrt(phases * mode_width)
    real_part = amplitude * jnp.cos(phases)
    imag_part = amplitude * jnp.sin(phases)
    upper_rows = jnp.concatenate([real_part, imag_part], axis=2)
    lower_rows = jnp.concatenate([-imag_part, real_part], axis=2)
    return jnp.concatenate([upper_rows, lower_rows], axis=1).astype(jnp.bfloat16)


def time_table(start_time, time_span):
    bin_numbers = F0 + jnp.arange(F, dtype=jnp.int32)
    sample_times = start_time + jnp.arange(time_span, dtype=jnp.int32)
    phase_turns = bin_numbers[:, None] * sample_times[None, :] % NT
    angles = phase_turns.astype(jnp.float32) * (2.0 * math.pi / NT)
    return jnp.stack([jnp.cos(angles), -jnp.sin(angles)], axis=1).astype(jnp.bfloat16)


def per_device(
    wavenumbers,
    receiver_shapes,
    source_shapes,
    mode_counts,
    source_depths,
    source_ranges,
    sections,
    recorded,
):
    freq_size = lax.axis_size("freq")
    sub_size = lax.axis_size("sub")
    freq_index = lax.axis_index("freq")
    sub_index = lax.axis_index("sub")
    local_count = sections.shape[0]
    stride = sub_size * local_count
    local_range = jnp.arange(local_count, dtype=jnp.int32)[None, :]
    bins_here = F // sub_size
    first_bin = sub_index * bins_here
    channel = (
        freq_index * stride
        + jnp.arange(sub_size, dtype=jnp.int32)[:, None] * local_count
        + local_range
    )
    positions = 1.0 + 2.0 * channel.reshape(-1).astype(jnp.float32) / R
    step_bins = math.gcd(bins_here, 4)
    step_count = bins_here // step_bins
    mode_width = wavenumbers.shape[1]
    depth_grid = source_shapes.shape[1]
    wave_steps = lax.dynamic_slice_in_dim(wavenumbers, first_bin, bins_here, 0).reshape(
        step_count, step_bins, mode_width
    )
    receiver_steps = lax.dynamic_slice_in_dim(receiver_shapes, first_bin, bins_here, 0).reshape(
        step_count, step_bins, mode_width
    )
    source_steps = lax.dynamic_slice_in_dim(source_shapes, first_bin, bins_here, 0).reshape(
        step_count, step_bins, depth_grid, mode_width
    )
    count_steps = lax.dynamic_slice_in_dim(mode_counts, first_bin, bins_here, 0).reshape(
        step_count, step_bins
    )

    def modal(inputs):
        wave_part, receiver_table, source_table, counts = inputs
        source_side = source_factor(wave_part, source_table, counts, source_depths, source_ranges)
        receiver_side = receiver_factor(wave_part, receiver_table, positions)
        return jnp.einsum(
            "bsk,bkn->bsn", source_side, receiver_side, preferred_element_type=jnp.float32
        ).astype(jnp.bfloat16)

    spectra = lax.map(modal, (wave_steps, receiver_steps, source_steps, count_steps))
    sources = source_depths.shape[0]
    spectra = spectra.reshape(bins_here, sources, 2, sub_size, local_count)
    norm_scale = 1.0 / math.sqrt(F)
    time_span = min(512, NT)
    exchanged = lax.all_to_all(spectra, "sub", split_axis=3, concat_axis=0, tiled=True)
    item_count = exchanged.shape[1]
    arranged = exchanged.reshape(F, item_count, 2, local_count)

    def one_span(start_time):
        dft_table = time_table(start_time, time_span)
        series = (
            jnp.einsum("fsqr,fqt->srt", arranged, dft_table, preferred_element_type=jnp.float32)
            * norm_scale
        )
        waveform = lax.dynamic_slice_in_dim(recorded, start_time, time_span, 1).astype(jnp.float32)
        return jnp.sum(jnp.tanh(series) * waveform[None, :, :], axis=2)

    span_starts = jnp.arange(NT // time_span, dtype=jnp.int32) * time_span
    matched = jnp.sum(lax.map(one_span, span_starts), axis=0)
    member = (sections[:, None] == jnp.arange(SEC, dtype=jnp.int32)[None, :]).astype(jnp.float32)
    partial_value = jnp.dot(matched, member, precision=lax.Precision.HIGHEST) * (
        1.0 / math.sqrt(NT * (R // SEC))
    )
    totals = lax.psum(partial_value, ("freq", "sub"))
    own_share = SEC // (freq_size * sub_size)
    return lax.dynamic_slice_in_dim(
        totals, (freq_index * sub_size + sub_index) * own_share, own_share, 1
    )


def solution(mesh):
    in_specs = (
        P(),
        P(),
        P(),
        P(),
        P("groups"),
        P("groups"),
        P(("freq", "sub")),
        P(("freq", "sub"), None),
    )
    out_specs = P("groups", ("freq", "sub"))
    return jax.shard_map(
        per_device, mesh=mesh, in_specs=in_specs, out_specs=out_specs, check_vma=False
    )
```

profile of v0, /device:TPU:0, one launch (start us, length us, event | category | flops | bytes accessed | tf_op | source)
XLA Modules:
  0.0 681.1 jit_solution(14347826808697491437)
XLA Ops:
  4.8 434.1 %while.24 = (s32[]{:T(128)}, bf16[32,4,16,1024]{3,2,1,0:T(8,128)(2,1)}, bf16[32,4,4,300]{3,2,1,0:T(4,128)(2,1)S(1)}, s32[16]{0:T(128)}, s32[32,4]{1,0:T(8,128)S(...) while((s32[]{:T(128)}, ...), condition=%wide.region_1.2_spmd.clone, body=%wide.region_0.1_spmd.clone.sunk | while | flops 104347648 | bytes 7718161 | solution.py:103
  6.1 10.2 %fusion.68 = (bf16[4,300,512]{2,1,0:T(8,128)(2,1)S(1)}, bf16[4,300,512]{2,1,0:T(8,128)(2,1)S(1)}, bf16[4,300,512]{2,1,0:T(8,128)(2,1)S(1)}) fusion(f32[512]{0:T(512)S(1)} %add_bitcast_fusion.2, f32[4,300]{1,0:T(4,128)S(1)} %get-tuple-element.301, f32[4,300]{1,0:T(4,128)S(1)} %get-tuple-element.302), kind=kLoop, calls=%fused_computation.40.clone.1 | loop fusion | flops 5529600 | bytes 3698048 | tf_op jit(solution)/shard_map/convert.5
  19.7 10.2 %fusion.68 = (bf16[4,300,512]{2,1,0:T(8,128)(2,1)S(1)}, bf16[4,300,512]{2,1,0:T(8,128)(2,1)S(1)}, bf16[4,300,512]{2,1,0:T(8,128)(2,1)S(1)}) fusion(f32[512]{0:T(512)S(1)} %add_bitcast_fusion.2, f32[4,300]{1,0:T(4,128)S(1)} %get-tuple-element.301, f32[4,300]{1,0:T(4,128)S(1)} %get-tuple-element.302), kind=kLoop, calls=%fused_computation.40.clone.1 | loop fusion | flops 5529600 | bytes 3698048 | tf_op jit(solution)/shard_map/convert.5
  33.3 10.2 %fusion.68 = (bf16[4,300,512]{2,1,0:T(8,128)(2,1)S(1)}, bf16[4,300,512]{2,1,0:T(8,128)(2,1)S(1)}, bf16[4,300,512]{2,1,0:T(8,128)(2,1)S(1)}) fusion(f32[512]{0:T(512)S(1)} %add_bitcast_fusion.2, f32[4,300]{1,0:T(4,128)S(1)} %get-tuple-element.301, f32[4,300]{1,0:T(4,128)S(1)} %get-tuple-element.302), kind=kLoop, calls=%fused_computation.40.clone.1 | loop fusion | flops 5529600 | bytes 3698048 | tf_op jit(solution)/shard_map/convert.5
  46.8 10.2 %fusion.68 = (bf16[4,300,512]{2,1,0:T(8,128)(2,1)S(1)}, bf16[4,300,512]{2,1,0:T(8,128)(2,1)S(1)}, bf16[4,300,512]{2,1,0:T(8,128)(2,1)S(1)}) fusion(f32[512]{0:T(512)S(1)} %add_bitcast_fusion.2, f32[4,300]{1,0:T(4,128)S(1)} %get-tuple-element.301, f32[4,300]{1,0:T(4,128)S(1)} %get-tuple-element.302), kind=kLoop, calls=%fused_computation.40.clone.1 | loop fusion | flops 5529600 | bytes 3698048 | tf_op jit(solution)/shard_map/convert.5
  60.4 10.2 %fusion.68 = (bf16[4,300,512]{2,1,0:T(8,128)(2,1)S(1)}, bf16[4,300,512]{2,1,0:T(8,128)(2,1)S(1)}, bf16[4,300,512]{2,1,0:T(8,128)(2,1)S(1)}) fusion(f32[512]{0:T(512)S(1)} %add_bitcast_fusion.2, f32[4,300]{1,0:T(4,128)S(1)} %get-tuple-element.301, f32[4,300]{1,0:T(4,128)S(1)} %get-tuple-element.302), kind=kLoop, calls=%fused_computation.40.clone.1 | loop fusion | flops 5529600 | bytes 3698048 | tf_op jit(solution)/shard_map/convert.5
  74.0 10.2 %fusion.68 = (bf16[4,300,512]{2,1,0:T(8,128)(2,1)S(1)}, bf16[4,300,512]{2,1,0:T(8,128)(2,1)S(1)}, bf16[4,300,512]{2,1,0:T(8,128)(2,1)S(1)}) fusion(f32[512]{0:T(512)S(1)} %add_bitcast_fusion.2, f32[4,300]{1,0:T(4,128)S(1)} %get-tuple-element.301, f32[4,300]{1,0:T(4,128)S(1)} %get-tuple-element.302), kind=kLoop, calls=%fused_computation.40.clone.1 | loop fusion | flops 5529600 | bytes 3698048 | tf_op jit(solution)/shard_map/convert.5
  87.5 10.2 %fusion.68 = (bf16[4,300,512]{2,1,0:T(8,128)(2,1)S(1)}, bf16[4,300,512]{2,1,0:T(8,128)(2,1)S(1)}, bf16[4,300,512]{2,1,0:T(8,128)(2,1)S(1)}) fusion(f32[512]{0:T(512)S(1)} %add_bitcast_fusion.2, f32[4,300]{1,0:T(4,128)S(1)} %get-tuple-element.301, f32[4,300]{1,0:T(4,128)S(1)} %get-tuple-element.302), kind=kLoop, calls=%fused_computation.40.clone.1 | loop fusion | flops 5529600 | bytes 3698048 | tf_op jit(solution)/shard_map/convert.5
  101.1 10.2 %fusion.68 = (bf16[4,300,512]{2,1,0:T(8,128)(2,1)S(1)}, bf16[4,300,512]{2,1,0:T(8,128)(2,1)S(1)}, bf16[4,300,512]{2,1,0:T(8,128)(2,1)S(1)}) fusion(f32[512]{0:T(512)S(1)} %add_bitcast_fusion.2, f32[4,300]{1,0:T(4,128)S(1)} %get-tuple-element.301, f32[4,300]{1,0:T(4,128)S(1)} %get-tuple-element.302), kind=kLoop, calls=%fused_computation.40.clone.1 | loop fusion | flops 5529600 | bytes 3698048 | tf_op jit(solution)/shard_map/convert.5
  114.6 10.2 %fusion.68 = (bf16[4,300,512]{2,1,0:T(8,128)(2,1)S(1)}, bf16[4,300,512]{2,1,0:T(8,128)(2,1)S(1)}, bf16[4,300,512]{2,1,0:T(8,128)(2,1)S(1)}) fusion(f32[512]{0:T(512)S(1)} %add_bitcast_fusion.2, f32[4,300]{1,0:T(4,128)S(1)} %get-tuple-element.301, f32[4,300]{1,0:T(4,128)S(1)} %get-tuple-element.302), kind=kLoop, calls=%fused_computation.40.clone.1 | loop fusion | flops 5529600 | bytes 3698048 | tf_op jit(solution)/shard_map/convert.5
  128.2 10.2 %fusion.68 = (bf16[4,300,512]{2,1,0:T(8,128)(2,1)S(1)}, bf16[4,300,512]{2,1,0:T(8,128)(2,1)S(1)}, bf16[4,300,512]{2,1,0:T(8,128)(2,1)S(1)}) fusion(f32[512]{0:T(512)S(1)} %add_bitcast_fusion.2, f32[4,300]{1,0:T(4,128)S(1)} %get-tuple-element.301, f32[4,300]{1,0:T(4,128)S(1)} %get-tuple-element.302), kind=kLoop, calls=%fused_computation.40.clone.1 | loop fusion | flops 5529600 | bytes 3698048 | tf_op jit(solution)/shard_map/convert.5
  141.8 10.2 %fusion.68 = (bf16[4,300,512]{2,1,0:T(8,128)(2,1)S(1)}, bf16[4,300,512]{2,1,0:T(8,128)(2,1)S(1)}, bf16[4,300,512]{2,1,0:T(8,128)(2,1)S(1)}) fusion(f32[512]{0:T(512)S(1)} %add_bitcast_fusion.2, f32[4,300]{1,0:T(4,128)S(1)} %get-tuple-element.301, f32[4,300]{1,0:T(4,128)S(1)} %get-tuple-element.302), kind=kLoop, calls=%fused_computation.40.clone.1 | loop fusion | flops 5529600 | bytes 3698048 | tf_op jit(solution)/shard_map/convert.5
  155.3 10.2 %fusion.68 = (bf16[4,300,512]{2,1,0:T(8,128)(2,1)S(1)}, bf16[4,300,512]{2,1,0:T(8,128)(2,1)S(1)}, bf16[4,300,512]{2,1,0:T(8,128)(2,1)S(1)}) fusion(f32[512]{0:T(512)S(1)} %add_bitcast_fusion.2, f32[4,300]{1,0:T(4,128)S(1)} %get-tuple-element.301, f32[4,300]{1,0:T(4,128)S(1)} %get-tuple-element.302), kind=kLoop, calls=%fused_computation.40.clone.1 | loop fusion | flops 5529600 | bytes 3698048 | tf_op jit(solution)/shard_map/convert.5
  168.9 10.2 %fusion.68 = (bf16[4,300,512]{2,1,0:T(8,128)(2,1)S(1)}, bf16[4,300,512]{2,1,0:T(8,128)(2,1)S(1)}, bf16[4,300,512]{2,1,0:T(8,128)(2,1)S(1)}) fusion(f32[512]{0:T(512)S(1)} %add_bitcast_fusion.2, f32[4,300]{1,0:T(4,128)S(1)} %get-tuple-element.301, f32[4,300]{1,0:T(4,128)S(1)} %get-tuple-element.302), kind=kLoop, calls=%fused_computation.40.clone.1 | loop fusion | flops 5529600 | bytes 3698048 | tf_op jit(solution)/shard_map/convert.5
  182.4 10.2 %fusion.68 = (bf16[4,300,512]{2,1,0:T(8,128)(2,1)S(1)}, bf16[4,300,512]{2,1,0:T(8,128)(2,1)S(1)}, bf16[4,300,512]{2,1,0:T(8,128)(2,1)S(1)}) fusion(f32[512]{0:T(512)S(1)} %add_bitcast_fusion.2, f32[4,300]{1,0:T(4,128)S(1)} %get-tuple-element.301, f32[4,300]{1,0:T(4,128)S(1)} %get-tuple-element.302), kind=kLoop, calls=%fused_computation.40.clone.1 | loop fusion | flops 5529600 | bytes 3698048 | tf_op jit(solution)/shard_map/convert.5
  196.0 10.2 %fusion.68 = (bf16[4,300,512]{2,1,0:T(8,128)(2,1)S(1)}, bf16[4,300,512]{2,1,0:T(8,128)(2,1)S(1)}, bf16[4,300,512]{2,1,0:T(8,128)(2,1)S(1)}) fusion(f32[512]{0:T(512)S(1)} %add_bitcast_fusion.2, f32[4,300]{1,0:T(4,128)S(1)} %get-tuple-element.301, f32[4,300]{1,0:T(4,128)S(1)} %get-tuple-element.302), kind=kLoop, calls=%fused_computation.40.clone.1 | loop fusion | flops 5529600 | bytes 3698048 | tf_op jit(solution)/shard_map/convert.5
  209.6 10.2 %fusion.68 = (bf16[4,300,512]{2,1,0:T(8,128)(2,1)S(1)}, bf16[4,300,512]{2,1,0:T(8,128)(2,1)S(1)}, bf16[4,300,512]{2,1,0:T(8,128)(2,1)S(1)}) fusion(f32[512]{0:T(512)S(1)} %add_bitcast_fusion.2, f32[4,300]{1,0:T(4,128)S(1)} %get-tuple-element.301, f32[4,300]{1,0:T(4,128)S(1)} %get-tuple-element.302), kind=kLoop, calls=%fused_computation.40.clone.1 | loop fusion | flops 5529600 | bytes 3698048 | tf_op jit(solution)/shard_map/convert.5
  223.1 10.2 %fusion.68 = (bf16[4,300,512]{2,1,0:T(8,128)(2,1)S(1)}, bf16[4,300,512]{2,1,0:T(8,128)(2,1)S(1)}, bf16[4,300,512]{2,1,0:T(8,128)(2,1)S(1)}) fusion(f32[512]{0:T(512)S(1)} %add_bitcast_fusion.2, f32[4,300]{1,0:T(4,128)S(1)} %get-tuple-element.301, f32[4,300]{1,0:T(4,128)S(1)} %get-tuple-element.302), kind=kLoop, calls=%fused_computation.40.clone.1 | loop fusion | flops 5529600 | bytes 3698048 | tf_op jit(solution)/shard_map/convert.5
  236.7 10.2 %fusion.68 = (bf16[4,300,512]{2,1,0:T(8,128)(2,1)S(1)}, bf16[4,300,512]{2,1,0:T(8,128)(2,1)S(1)}, bf16[4,300,512]{2,1,0:T(8,128)(2,1)S(1)}) fusion(f32[512]{0:T(512)S(1)} %add_bitcast_fusion.2, f32[4,300]{1,0:T(4,128)S(1)} %get-tuple-element.301, f32[4,300]{1,0:T(4,128)S(1)} %get-tuple-element.302), kind=kLoop, calls=%fused_computation.40.clone.1 | loop fusion | flops 5529600 | bytes 3698048 | tf_op jit(solution)/shard_map/convert.5
  250.3 10.2 %fusion.68 = (bf16[4,300,512]{2,1,0:T(8,128)(2,1)S(1)}, bf16[4,300,512]{2,1,0:T(8,128)(2,1)S(1)}, bf16[4,300,512]{2,1,0:T(8,128)(2,1)S(1)}) fusion(f32[512]{0:T(512)S(1)} %add_bitcast_fusion.2, f32[4,300]{1,0:T(4,128)S(1)} %get-tuple-element.301, f32[4,300]{1,0:T(4,128)S(1)} %get-tuple-element.302), kind=kLoop, calls=%fused_computation.40.clone.1 | loop fusion | flops 5529600 | bytes 3698048 | tf_op jit(solution)/shard_map/convert.5
  263.8 10.2 %fusion.68 = (bf16[4,300,512]{2,1,0:T(8,128)(2,1)S(1)}, bf16[4,300,512]{2,1,0:T(8,128)(2,1)S(1)}, bf16[4,300,512]{2,1,0:T(8,128)(2,1)S(1)}) fusion(f32[512]{0:T(512)S(1)} %add_bitcast_fusion.2, f32[4,300]{1,0:T(4,128)S(1)} %get-tuple-element.301, f32[4,300]{1,0:T(4,128)S(1)} %get-tuple-element.302), kind=kLoop, calls=%fused_computation.40.clone.1 | loop fusion | flops 5529600 | bytes 3698048 | tf_op jit(solution)/shard_map/convert.5
  277.4 10.2 %fusion.68 = (bf16[4,300,512]{2,1,0:T(8,128)(2,1)S(1)}, bf16[4,300,512]{2,1,0:T(8,128)(2,1)S(1)}, bf16[4,300,512]{2,1,0:T(8,128)(2,1)S(1)}) fusion(f32[512]{0:T(512)S(1)} %add_bitcast_fusion.2, f32[4,300]{1,0:T(4,128)S(1)} %get-tuple-element.301, f32[4,300]{1,0:T(4,128)S(1)} %get-tuple-element.302), kind=kLoop, calls=%fused_computation.40.clone.1 | loop fusion | flops 5529600 | bytes 3698048 | tf_op jit(solution)/shard_map/convert.5
  291.0 10.2 %fusion.68 = (bf16[4,300,512]{2,1,0:T(8,128)(2,1)S(1)}, bf16[4,300,512]{2,1,0:T(8,128)(2,1)S(1)}, bf16[4,300,512]{2,1,0:T(8,128)(2,1)S(1)}) fusion(f32[512]{0:T(512)S(1)} %add_bitcast_fusion.2, f32[4,300]{1,0:T(4,128)S(1)} %get-tuple-element.301, f32[4,300]{1,0:T(4,128)S(1)} %get-tuple-element.302), kind=kLoop, calls=%fused_computation.40.clone.1 | loop fusion | flops 5529600 | bytes 3698048 | tf_op jit(solution)/shard_map/convert.5
  304.5 10.2 %fusion.68 = (bf16[4,300,512]{2,1,0:T(8,128)(2,1)S(1)}, bf16[4,300,512]{2,1,0:T(8,128)(2,1)S(1)}, bf16[4,300,512]{2,1,0:T(8,128)(2,1)S(1)}) fusion(f32[512]{0:T(512)S(1)} %add_bitcast_fusion.2, f32[4,300]{1,0:T(4,128)S(1)} %get-tuple-element.301, f32[4,300]{1,0:T(4,128)S(1)} %get-tuple-element.302), kind=kLoop, calls=%fused_computation.40.clone.1 | loop fusion | flops 5529600 | bytes 3698048 | tf_op jit(solution)/shard_map/convert.5
  318.1 10.2 %fusion.68 = (bf16[4,300,512]{2,1,0:T(8,128)(2,1)S(1)}, bf16[4,300,512]{2,1,0:T(8,128)(2,1)S(1)}, bf16[4,300,512]{2,1,0:T(8,128)(2,1)S(1)}) fusion(f32[512]{0:T(512)S(1)} %add_bitcast_fusion.2, f32[4,300]{1,0:T(4,128)S(1)} %get-tuple-element.301, f32[4,300]{1,0:T(4,128)S(1)} %get-tuple-element.302), kind=kLoop, calls=%fused_computation.40.clone.1 | loop fusion | flops 5529600 | bytes 3698048 | tf_op jit(solution)/shard_map/convert.5
  345.2 10.2 %fusion.68 = (bf16[4,300,512]{2,1,0:T(8,128)(2,1)S(1)}, bf16[4,300,512]{2,1,0:T(8,128)(2,1)S(1)}, bf16[4,300,512]{2,1,0:T(8,128)(2,1)S(1)}) fusion(f32[512]{0:T(512)S(1)} %add_bitcast_fusion.2, f32[4,300]{1,0:T(4,128)S(1)} %get-tuple-element.301, f32[4,300]{1,0:T(4,128)S(1)} %get-tuple-element.302), kind=kLoop, calls=%fused_computation.40.clone.1 | loop fusion | flops 5529600 | bytes 3698048 | tf_op jit(solution)/shard_map/convert.5
  358.8 10.2 %fusion.68 = (bf16[4,300,512]{2,1,0:T(8,128)(2,1)S(1)}, bf16[4,300,512]{2,1,0:T(8,128)(2,1)S(1)}, bf16[4,300,512]{2,1,0:T(8,128)(2,1)S(1)}) fusion(f32[512]{0:T(512)S(1)} %add_bitcast_fusion.2, f32[4,300]{1,0:T(4,128)S(1)} %get-tuple-element.301, f32[4,300]{1,0:T(4,128)S(1)} %get-tuple-element.302), kind=kLoop, calls=%fused_computation.40.clone.1 | loop fusion | flops 5529600 | bytes 3698048 | tf_op jit(solution)/shard_map/convert.5
  385.9 10.2 %fusion.68 = (bf16[4,300,512]{2,1,0:T(8,128)(2,1)S(1)}, bf16[4,300,512]{2,1,0:T(8,128)(2,1)S(1)}, bf16[4,300,512]{2,1,0:T(8,128)(2,1)S(1)}) fusion(f32[512]{0:T(512)S(1)} %add_bitcast_fusion.2, f32[4,300]{1,0:T(4,128)S(1)} %get-tuple-element.301, f32[4,300]{1,0:T(4,128)S(1)} %get-tuple-element.302), kind=kLoop, calls=%fused_computation.40.clone.1 | loop fusion | flops 5529600 | bytes 3698048 | tf_op jit(solution)/shard_map/convert.5
  426.6 10.2 %fusion.68 = (bf16[4,300,512]{2,1,0:T(8,128)(2,1)S(1)}, bf16[4,300,512]{2,1,0:T(8,128)(2,1)S(1)}, bf16[4,300,512]{2,1,0:T(8,128)(2,1)S(1)}) fusion(f32[512]{0:T(512)S(1)} %add_bitcast_fusion.2, f32[4,300]{1,0:T(4,128)S(1)} %get-tuple-element.301, f32[4,300]{1,0:T(4,128)S(1)} %get-tuple-element.302), kind=kLoop, calls=%fused_computation.40.clone.1 | loop fusion | flops 5529600 | bytes 3698048 | tf_op jit(solution)/shard_map/convert.5
  459.0 48.8 %all-to-all-done = bf16[128,16,2,4,128]{4,2,1,0,3:T(2,128)(2,1)} async-done(((bf16[128,16,2,4,128]{4,2,1,0,3:T(2,128)(2,1)}), bf16[128,16,2,4,128]{4,2,1,0,3:T(2,128)(2,1)}, u32[]{:S(2)}, u32[]{:S(2)}) %all-to-all-start) | async-done | bytes 4194336 | tf_op jit(solution)/shard_map/all_to_all | solution.py:108
  513.6 105.6 %while.23 = (s32[]{:T(128)}, f32[8,16,128]{2,1,0:T(8,128)S(1)}, s32[8]{0:T(128)S(1)}, bf16[512,16,2,128]{3,0,2,1:T(8,128)(2,1)}, bf16[128,4096]{1,0:T(8,128)(2,1)}, /*index=5*/s32[]{:T(128)}, s32[]{:T(128)}, s32[]{:T(128)}) while((s32[]{:T(128)}, f32[8,16,128]{2,1,0:T(8,128)S(1)}, s32[8]{0:T(128)S(1)}, bf16[512,16,2,128]{3,0,2,1:T(8,128)(2,1)}, ...), condition=%wide.region_4.5_spmd, body=%wide.region_2.4_spmd.sunk | while | flops 2157247488 | bytes 7504015 | solution.py:122
  619.6 60.9 %psum.7 = f32[16,512]{1,0:T(8,128)S(1)} all-reduce(f32[16,512]{1,0:T(8,128)S(1)} %convolution_multiply_fusion.1), channel_id=1, replica_groups=mesh['groups'=2,'freq'=4,'sub'=4] {'freq','sub'}, use_global_device_ids=true, to_apply=%region_6.7 | all-reduce | flops 8192 | bytes 65536 | tf_op jit(solution)/shard_map/psum | solution.py:127
  (285 shorter events, 269.8 us)
Async XLA Ops:
  0.0 1.3 copy-start
  454.0 53.9 %all-to-all-start = ((bf16[128,16,2,4,128]{4,2,1,0,3:T(2,128)(2,1)}), bf16[128,16,2,4,128]{4,2,1,0,3:T(2,128)(2,1)}, u32[]{:S(2)}, u32[]{:S(2)}) async-start(bf16[128,16,2,4,128]{4,2,1,0,3:T(2,128)(2,1)} %copy.27), calls=%async_computation | async-start | bytes 8388608 | tf_op jit(solution)/shard_map/all_to_all | solution.py:108
  513.6 105.7 %copy-start.1 = (s32[128]{0:T(128)S(1)}, s32[128]{0:T(128)}, u32[]{:S(2)}) copy-start(s32[128]{0:T(128)} %param.18) | copy-start | bytes 1540
where the time goes:
time: 683 us; the launch traced here: 681 us
  other arithmetic  374 us (55%)
  matrix products  137 us (20%)
  blocking collectives  60.9 us (9%)
  waiting for transfers between devices  48.8 us (7%)
  local copies, waits for them, and re-layouts  40.2 us (6%)
  loops' own time  14.7 us (2%)
    another operation x40, other arithmetic  364 us
    dot_general x32, matrix products, modal(): jnp.einsum('bsk,bkn->bsn', source_side, receiver_side, preferred_element_...  64.5 us
    psum x1, blocking collectives, per_device(): totals = lax.psum(partial_value, ('freq', 'sub'))  60.9 us
    all_to_all x1, waiting for transfers between devices, per_device(): lax.all_to_all(spectra, 'sub', split_axis=3, concat_axis=0, tiled=True)  48.8 us
    dot_general x8, matrix products, one_span(): jnp.einsum('fsqr,fqt->srt', arranged, dft_table, preferred_element_type=j...  36.3 us
    dot_general x32, matrix products, source_factor(): jnp.einsum('sz,bzm->bsm', chooser, source_table.astype(jnp.float32), prec...  36.3 us
    reshape x2, local copies, waits for them, and re-layouts, per_device(): spectra = spectra.reshape(bins_here, sources, 2, sub_size, local_count)  15.1 us
    another operation x1, loops' own time, per_device(): matched = jnp.sum(lax.map(one_span, span_starts), axis=0)  14.2 us
  transfers between devices with their start and end apart: 1, of which 1 were waited for; matrix products, arithmetic and copies ran while one was open for 0% of the time, Pallas kernels for 0%

commit v1 on v0

v1 whole, which is shorter than its diff:
```python
import functools
import math

import jax
import jax.numpy as jnp
import numpy as np
from jax import lax
from jax.experimental import pallas as pl
from jax.experimental.pallas import tpu as pltpu
from jax.sharding import PartitionSpec as P

MMIN = 64
F0 = 256
SPREAD = 16
K_LOW, K_TOP = 1.0, 20.0
R_TOP = 0.5
K_MID, K_HALF = 0.5 * (K_LOW + K_TOP), 0.5 * (K_TOP - K_LOW)
LANES = 128
TERMS = 16
TWO_PI = 2.0 * math.pi


def sincos_turns(turns):
    part = turns - jnp.floor(turns + 0.5)
    sq = part * part
    p2 = math.pi * math.pi
    s = jnp.full_like(part, -(p2**5) / math.factorial(11))
    for n in (9, 7, 5, 3, 1):
        s = s * sq + ((-1) ** ((n - 1) // 2)) * p2 ** ((n - 1) // 2) / math.factorial(n)
    s = s * (part * math.pi)
    c = jnp.full_like(part, p2**6 / math.factorial(12))
    for n in (10, 8, 6, 4, 2, 0):
        c = c * sq + ((-1) ** (n // 2)) * p2 ** (n // 2) / math.factorial(n)
    return 1.0 - 2.0 * s * s, 2.0 * s * c


def term_constants():
    nodes = np.cos(np.pi * (np.arange(TERMS) + 0.5) / TERMS)[: TERMS // 2]
    order = np.arange(TERMS)
    table = np.cos(order[:, None] * np.arccos(nodes)[None, :])
    table *= (np.where(order == 0, 1.0, 2.0) * 2.0 / TERMS)[:, None]
    half = TERMS // 2
    out = np.zeros((half, LANES), np.float32)
    out[:, 0] = K_HALF * nodes
    out[:, 1 : 1 + half] = table[0::2]
    out[:, 1 + half : 1 + 2 * half] = table[1::2]
    return out


def place_of(n):
    return n // 2 if n % 2 == 0 else TERMS // 2 + n // 2


def tile_groups(bins, modes, per_group):
    runs = []
    for group in range(bins // per_group):
        last = (group + 1) * per_group - 1
        top = min(modes, MMIN + (modes - MMIN) * last // max(bins - 1, 1) + SPREAD)
        tiles = -(-top // LANES)
        if runs and runs[-1][2] == tiles:
            runs[-1][1] = group + 1
        else:
            runs.append([group, group + 1, tiles])
    return runs


def replica_kernel(
    shape,
    depths_ref,
    place_ref,
    ranges_ref,
    consts_ref,
    wave_ref,
    ampl_ref,
    recorded_ref,
    out_ref,
    re_ref,
    im_ref,
    tab_ref,
    part_ref,
    psi_ref,
    coef_ref,
):
    bins, modes, depth_grid, sources, channels, samples, receivers = shape
    quarter = bins // 4
    span = samples // 4
    half = TERMS // 2
    first_x = place_ref[0]
    centre = place_ref[1]

    def modal(start, tiles):
        rows = pl.ds(pl.multiple_of(start, 8), 8)
        cols = pl.ds(0, tiles * LANES)
        wave = wave_ref[rows, cols]
        cosine, sine = sincos_turns(wave * (centre * (1.0 / TWO_PI)))
        xi = (wave - K_MID) * (1.0 / K_HALF)
        twice = xi + xi
        parts = []
        for z in range(depth_grid):
            ampl = ampl_ref[z, rows, cols]
            parts.append((ampl * cosine, ampl * sine))
        lane = lax.broadcasted_iota(jnp.int32, (8, LANES), 1)
        total = jnp.zeros((8, LANES), jnp.float32)
        before, now = None, None
        for n in range(TERMS):
            if n == 1:
                before, now = jnp.ones_like(xi), xi
            elif n > 1:
                before, now = now, twice * now - before
            for z in range(depth_grid):
                for c in range(2):
                    product = parts[z][c] if n == 0 else parts[z][c] * now
                    folded = product[:, :LANES]
                    for tile in range(1, tiles):
                        folded = folded + product[:, tile * LANES : (tile + 1) * LANES]
                    value = jnp.sum(folded, axis=1, keepdims=True)
                    at = z * 2 * TERMS + c * TERMS + place_of(n)
                    total = jnp.where(lane == at, value, total)
        real_lane = lane % (2 * TERMS) < TERMS
        swapped = jnp.where(
            real_lane, pltpu.roll(total, LANES - TERMS, 1), -pltpu.roll(total, TERMS, 1)
        )
        re_ref[rows, :] = total
        im_ref[rows, :] = swapped

    for first, last, tiles in tile_groups(bins, modes, 32):

        def body(i, carry, first=first, last=last, tiles=tiles):
            count = last - first
            modal((i // count) * quarter + (first + i % count) * 8, tiles)
            return carry

        lax.fori_loop(0, 4 * (last - first), body, 0)

    for r in range(4):
        row = lax.broadcasted_iota(jnp.int32, (quarter, LANES), 0)
        column = lax.broadcasted_iota(jnp.int32, (quarter, LANES), 1)
        number = F0 + 4 * row + r
        whole = (number * column) % samples
        cosine, sine = sincos_turns(whole.astype(jnp.float32) * (1.0 / samples))
        turn = (number * LANES) % samples
        step_c, step_s = sincos_turns(turn.astype(jnp.float32) * (1.0 / samples))
        for block in range(span // LANES):
            cols = slice(block * LANES, (block + 1) * LANES)
            tab_ref[:quarter, cols] = cosine.astype(jnp.bfloat16)
            tab_ref[quarter:, cols] = (-sine).astype(jnp.bfloat16)
            cosine, sine = cosine * step_c - sine * step_s, cosine * step_s + sine * step_c
        rows = slice(r * quarter, (r + 1) * quarter)
        left = jnp.concatenate([re_ref[rows, :].T, im_ref[rows, :].T], axis=1)
        part_ref[r] = jnp.dot(
            left.astype(jnp.bfloat16), tab_ref[...], preferred_element_type=jnp.float32
        )

    def times_i(value):
        blocks = []
        for z in range(depth_grid):
            base = z * 2 * TERMS
            blocks.append(-value[base + TERMS : base + 2 * TERMS])
            blocks.append(value[base : base + TERMS])
        return jnp.concatenate(blocks, axis=0)

    for block in range(span // LANES):
        cols = slice(block * LANES, (block + 1) * LANES)
        p0, p1, p2, p3 = (part_ref[r, :, cols] for r in range(4))
        even, odd = p0 + p2, p1 + p3
        gap, turned = p0 - p2, times_i(p1 - p3)
        for q, value in enumerate((even + odd, gap + turned, even - odd, gap - turned)):
            at = q * span + block * LANES
            psi_ref[:, at : at + LANES] = value.astype(jnp.bfloat16)

    channel = lax.broadcasted_iota(jnp.int32, (1, channels), 1).astype(jnp.float32)
    position = first_x + channel * (2.0 / receivers)
    spread = lax.rsqrt(position)
    nodes = consts_ref[:, 0:1]
    for s in range(sources):
        offset = position - (ranges_ref[s] + centre)
        cosine, sine = sincos_turns(nodes * offset * (1.0 / TWO_PI))
        even = jnp.zeros((half, channels), jnp.float32)
        odd = jnp.zeros((half, channels), jnp.float32)
        for j in range(half):
            even = even + consts_ref[:, 1 + j : 2 + j] * cosine[j : j + 1, :]
            odd = odd + consts_ref[:, 1 + half + j : 2 + half + j] * sine[j : j + 1, :]
        mid_c, mid_s = sincos_turns(offset * (K_MID / TWO_PI))
        mid_c, mid_s = mid_c * spread, mid_s * spread
        rows = jnp.concatenate([mid_c * even, -mid_s * odd, -mid_s * even, -mid_c * odd], axis=0)
        coef_ref[s] = rows.T.astype(jnp.bfloat16)

    chunk = 512

    def source(s, matched):
        z = depths_ref[s]
        terms = pl.ds(pl.multiple_of(z * (2 * TERMS), 2 * TERMS), 2 * TERMS)
        coef = coef_ref[s]
        total = jnp.zeros((channels, LANES), jnp.float32)
        for start in range(0, samples, chunk):
            series = jnp.dot(
                coef, psi_ref[terms, start : start + chunk], preferred_element_type=jnp.float32
            )
            product = jnp.tanh(series) * recorded_ref[:, start : start + chunk].astype(jnp.float32)
            for tile in range(chunk // LANES):
                total = total + product[:, tile * LANES : (tile + 1) * LANES]
        value = jnp.sum(total, axis=1, keepdims=True)
        lane = lax.broadcasted_iota(jnp.int32, (channels, LANES), 1)
        return jnp.where(lane == s, value, matched)

    out_ref[...] = lax.fori_loop(
        0, sources, source, jnp.zeros((channels, LANES), jnp.float32)
    )


def exchange_kernel(sizes, block_ref, out_ref, held_ref, send_sem, recv_sem):
    freq_size, sub_size = sizes
    count = freq_size * sub_size
    me = lax.axis_index("freq") * sub_size + lax.axis_index("sub")
    barrier = pltpu.get_barrier_semaphore()

    def place(number):
        return {"freq": number // sub_size, "sub": number % sub_size}

    def greet(i, carry):
        pl.semaphore_signal(
            barrier,
            inc=1,
            device_id=place((me + i) % count),
            device_id_type=pl.DeviceIdType.MESH,
        )
        return carry

    lax.fori_loop(1, count, greet, 0)
    pl.semaphore_wait(barrier, count - 1)

    def copy_to(target, source):
        return pltpu.make_async_remote_copy(
            src_ref=block_ref.at[target],
            dst_ref=held_ref.at[source],
            send_sem=send_sem.at[target],
            recv_sem=recv_sem.at[source],
            device_id=place(target),
            device_id_type=pl.DeviceIdType.MESH,
        )

    def send(i, carry):
        copy_to((me + i) % count, me).start()
        return carry

    lax.fori_loop(1, count, send, 0)

    def receive(i, total):
        source = (me + count - i) % count
        copy_to(source, source).wait_recv()
        return total + held_ref[source]

    out_ref[...] = lax.fori_loop(1, count, receive, block_ref[me])

    def drain(i, carry):
        copy_to((me + i) % count, me).wait_send()
        return carry

    lax.fori_loop(1, count, drain, 0)


def per_device(
    mesh_sizes,
    wavenumbers,
    receiver_shapes,
    source_shapes,
    mode_counts,
    source_depths,
    source_ranges,
    sections,
    recorded,
):
    freq_size, sub_size = mesh_sizes
    count = freq_size * sub_size
    me = lax.axis_index("freq") * sub_size + lax.axis_index("sub")
    bins, modes = wavenumbers.shape
    depth_grid = source_shapes.shape[1]
    sources = source_depths.shape[0]
    channels, samples = recorded.shape
    receivers = channels * count
    width = -(-modes // LANES) * LANES

    first_x = 1.0 + 2.0 * (me * channels).astype(jnp.float32) / receivers
    reach = 2.0 * (channels - 1) / receivers
    centre = first_x + 0.5 * (reach - R_TOP)
    top_phase = K_HALF * 0.5 * (reach + R_TOP)
    assert 2.0 * (0.5 * top_phase) ** TERMS / math.factorial(TERMS) < 1e-9
    assert depth_grid * 2 * TERMS <= LANES

    def regroup(value, fill):
        value = jnp.pad(value, [(0, 0)] * (value.ndim - 1) + [(0, width - modes)], constant_values=fill)
        shape = value.shape
        value = value.reshape(shape[:-2] + (bins // 4, 4, width))
        return jnp.swapaxes(value, -3, -2).reshape(shape)

    wave = wavenumbers
    live = jnp.arange(modes, dtype=jnp.int32)[None, :] < mode_counts[:, None]
    factor = receiver_shapes.astype(jnp.float32) * (8.0 / math.sqrt(bins))
    factor = jnp.where(live, factor / jnp.sqrt(wave * modes), 0.0)
    ampl = jnp.swapaxes(source_shapes, 0, 1).astype(jnp.float32) * factor[None]
    ampl = jnp.pad(ampl, ((0, LANES // (2 * TERMS) - depth_grid), (0, 0), (0, 0)))
    shape = (bins, modes, LANES // (2 * TERMS), sources, channels, samples, receivers)
    matched = pl.pallas_call(
        functools.partial(replica_kernel, shape),
        out_shape=jax.ShapeDtypeStruct((channels, LANES), jnp.float32),
        in_specs=[pl.BlockSpec(memory_space=pltpu.SMEM)] * 3
        + [pl.BlockSpec(memory_space=pltpu.VMEM)] * 4,
        out_specs=pl.BlockSpec(memory_space=pltpu.VMEM),
        scratch_shapes=[
            pltpu.VMEM((bins, LANES), jnp.float32),
            pltpu.VMEM((bins, LANES), jnp.float32),
            pltpu.VMEM((bins // 2, samples // 4), jnp.bfloat16),
            pltpu.VMEM((4, LANES, samples // 4), jnp.float32),
            pltpu.VMEM((LANES, samples), jnp.bfloat16),
            pltpu.VMEM((sources, channels, 2 * TERMS), jnp.bfloat16),
        ],
        compiler_params=pltpu.CompilerParams(vmem_limit_bytes=48 * 1024 * 1024),
        name="replica",
    )(
        source_depths,
        jnp.stack([first_x, centre]),
        source_ranges,
        jnp.asarray(term_constants()),
        regroup(wave, K_MID),
        regroup(ampl, 0.0),
        recorded,
    )

    section_count = receivers // 4
    own = section_count // count
    padded = -(-own // 8) * 8
    slot = jnp.arange(count * padded, dtype=jnp.int32)
    wanted = jnp.where(slot % padded < own, slot // padded * own + slot % padded, -1)
    member = (wanted[:, None] == sections[None, :]).astype(jnp.float32)
    blocks = jnp.dot(member, matched, precision=lax.Precision.HIGHEST) * (
        1.0 / math.sqrt(samples * (receivers // section_count))
    )
    blocks = blocks.reshape(count, padded, LANES)
    total = pl.pallas_call(
        functools.partial(exchange_kernel, (freq_size, sub_size)),
        out_shape=jax.ShapeDtypeStruct((padded, LANES), jnp.float32),
        in_specs=[pl.BlockSpec(memory_space=pltpu.VMEM)],
        out_specs=pl.BlockSpec(memory_space=pltpu.VMEM),
        scratch_shapes=[
            pltpu.VMEM((count, padded, LANES), jnp.float32),
            pltpu.SemaphoreType.DMA((count,)),
            pltpu.SemaphoreType.DMA((count,)),
        ],
        compiler_params=pltpu.CompilerParams(collective_id=0, has_side_effects=True),
        name="exchange",
    )(blocks)
    return total[:own, :sources].T


def solution(mesh):
    sizes = (mesh.shape["freq"], mesh.shape["sub"])
    in_specs = (
        P(),
        P(),
        P(),
        P(),
        P("groups"),
        P("groups"),
        P(("freq", "sub")),
        P(("freq", "sub"), None),
    )
    out_specs = P("groups", ("freq", "sub"))
    return jax.shard_map(
        functools.partial(per_device, sizes),
        mesh=mesh,
        in_specs=in_specs,
        out_specs=out_specs,
        check_vma=False,
    )
```

time: 683 us -> 64.7 us (0.09)
  other arithmetic: 374 us -> 4.76 us
  matrix products: 137 us -> 1.02 us
  blocking collectives: 60.9 us -> 0 us
  waiting for transfers between devices: 48.8 us -> 0 us
  Pallas kernels: 0 us -> 43.2 us
  local copies, waits for them, and re-layouts: 40.2 us -> 15.2 us
  loops' own time: 14.7 us -> 0 us
    another operation x40 -> x1, other arithmetic: 364 us -> 0.07 us  [per_device(): jnp.stack([first_x, centre])]
    dot_general x73 -> x1, matrix products: 137 us -> 1.02 us  [per_device(): jnp.dot(member, matched, precision=lax.Precision.HIGHEST)]
    psum x1 -> x0, blocking collectives: 60.9 us -> none  [per_device(): totals = lax.psum(partial_value, ('freq', 'sub'))]
    all_to_all x1 -> x0, waiting for transfers between devices: 48.8 us -> none  [per_device(): lax.all_to_all(spectra, 'sub', split_axis=3, concat_axis=0, tiled=True)]
    pallas_call x0 -> x2, Pallas kernels: none -> 43.2 us  [the longest x1 30.6 us: per_device(): pl.pallas_call(functools.partial(replica_kernel, shape), out_shape=jax.Sh...]
    dynamic_slice x32 -> x0, local copies, waits for them, and re-layouts: 17.7 us -> none  [the longest x16 9.13 us: one_span(): lax.dynamic_slice_in_dim(recorded, start_time, time_span, 1)]
    another operation x2 -> x0, loops' own time: 14.7 us -> none  [the longest x1 14.2 us: per_device(): matched = jnp.sum(lax.map(one_span, span_starts), axis=0)]
    reshape x5 -> x1, local copies, waits for them, and re-layouts: 15.3 us -> 2.26 us  [regroup(): value = value.reshape(shape[:-2] + (bins // 4, 4, width))]
  transfers between devices with their start and end apart: 1 -> 0, of which waited for: 1 -> 0; matrix products, arithmetic and copies ran while one was open for 0% -> 0% of each run, Pallas kernels for 0% -> 0%
where the time goes in v1:
time: 64.7 us; the launch traced here: 64.2 us
  Pallas kernels  43.2 us (67%)
  local copies, waits for them, and re-layouts  15.2 us (23%)
  other arithmetic  4.76 us (7%)
  matrix products  1.02 us (2%)
    pallas_call x1, Pallas kernels, per_device(): pl.pallas_call(functools.partial(replica_kernel, shape), out_shape=jax.Sh...  30.6 us
    pallas_call x1, Pallas kernels, per_device(): pl.pallas_call(functools.partial(exchange_kernel, (freq_size, sub_size)),...  12.6 us
    unnamed x12, local copies, waits for them, and re-layouts  6.68 us
    mul x1, other arithmetic, per_device(): ampl = jnp.swapaxes(source_shapes, 0, 1).astype(jnp.float32) * factor[None]  3.36 us
    pad x2, local copies, waits for them, and re-layouts, regroup(): jnp.pad(value, [(0, 0)] * (value.ndim - 1) + [(0, width - modes)], consta...  2.66 us
    reshape x1, local copies, waits for them, and re-layouts, regroup(): value = value.reshape(shape[:-2] + (bins // 4, 4, width))  2.26 us
    transpose x2, local copies, waits for them, and re-layouts, regroup(): return jnp.swapaxes(value, -3, -2).reshape(shape)  2.2 us
    transpose x2, local copies, waits for them, and re-layouts, per_device(): return total[:own, :sources].T  1.39 us

profile of v1, /device:TPU:0, one launch (start us, length us, event | category | flops | bytes accessed | tf_op | source)
XLA Modules:
  0.0 64.2 jit_solution(2491359944503428057)
XLA Ops:
  0.0 0.1 pad_maximum_fusion.place_ref
  0.1 1.3 %multiply_select_fusion = f32[512,300]{0,1:T(8,128)S(1)} fusion(f32[512,300]{0,1:T(8,128)} %param.9, bf16[512,300]{0,1:T(8,128)(2,1)} %param.10, s32[512]{0:T(512)} %param.12), kind=kLoop, calls=%fused_computation.2 | loop fusion | flops 921600 | bytes 1538048 | tf_op jit(solution)/shard_map/jit(_where)/select_n | solution.py:299
  1.4 3.4 %multiply_bitcast_fusion = f32[4,512,300]{1,0,2:T(4,128)} fusion(bf16[512,4,300]{0,1,2:T(4,128)(2,1)} %param.11, f32[512,300]{0,1:T(8,128)S(1)} %multiply_select_fusion), kind=kLoop, calls=%fused_computation | loop fusion | flops 1228800 | bytes 4300800 | tf_op jit(solution)/shard_map/mul | solution.py:300
  4.8 3.2 %copy.19 = f32[4,512,300]{2,0,1:T(4,128)S(1)} copy(f32[4,512,300]{1,0,2:T(4,128)} %multiply_bitcast_fusion) | data formatting | bytes 4915200
  8.0 0.5 pad.9.clone
  8.5 1.0 %copy.16 = f32[4,4,128,384]{3,2,1,0:T(8,128)S(1)} copy(f32[4,4,128,384]{3,0,1,2:T(4,128)S(1)} %bitcast.16) | data formatting | bytes 6291456 | tf_op jit(solution)/shard_map/transpose | solution.py:294
  9.5 2.2 %copy.18 = f32[512,300]{1,0:T(8,128)} copy(f32[512,300]{0,1:T(8,128)} %param.9) | data formatting | bytes 1228800
  11.8 0.0 copy-start.1
  11.8 0.0 copy-start.2
  11.8 0.0 copy-start.3
  11.8 2.1 %pad.8.clone = f32[512,384]{1,0:T(8,128)} pad(f32[512,300]{1,0:T(8,128)} %copy.18, f32[]{:T(128)} %constant.65.clone.1), padding=0_0x0_84 | pad | bytes 1400836 | tf_op jit(solution)/shard_map/jit(_pad)/pad | solution.py:291
  13.9 2.3 %reshape.42 = f32[128,4,384]{2,1,0:T(4,128)} reshape(f32[512,384]{1,0:T(8,128)} %pad.8.clone) | data formatting | bytes 1572864 | tf_op jit(solution)/shard_map/reshape | solution.py:293
  16.2 1.2 %copy.14 = f32[4,128,384]{2,1,0:T(8,128)S(1)} copy(f32[4,128,384]{2,0,1:T(4,128)} %bitcast.17) | data formatting | bytes 1572864 | tf_op jit(solution)/shard_map/transpose | solution.py:294
  17.3 0.0 copy-done.1
  17.4 0.0 copy-done.2
  17.4 0.0 copy-done.3
  17.4 0.0 copy-start
  17.4 1.2 %copy-done = bf16[128,4096]{1,0:T(8,128)(2,1)S(1)} copy-done((bf16[128,4096]{1,0:T(8,128)(2,1)S(1)}, bf16[128,4096]{1,0:T(8,128)(2,1)}, u32[]{:S(2)}) %copy-start) | copy-done | bytes 1048600
  18.6 0.0 copy-start.4
  18.6 30.6 %replica.1 = f32[128,128]{1,0:T(8,128)S(1)} custom-call(s32[16]{0:T(128)S(1)} %copy-done.2, f32[2]{0:T(128)S(1)} %pad_maximum_fusion.place_ref, f32[16]{0:T(128)S(1)} %copy-done.3, f32[8,128]{1,0:T(8,128)S(1)} %copy-done.1, f32[512,384]{1,0:T(8,128)S(1)} %bitcast.15, f32[4,512,384]{2,1,0:T(8,128)S(1)} %bitcast.14, bf16[128,4096]{1,0:T(8,128)(2,1)S(1)} %copy-done), custom_call_target="tpu_custom_call" | custom-call | tf_op jit(solution)/shard_map/replica/pallas_call | solution.py:303
  49.2 0.0 copy-done.4
  49.2 1.0 %convolution_multiply_fusion = f32[512,128]{1,0:T(8,128)} fusion(f32[128,128]{1,0:T(8,128)S(1)} %replica.1, s32[128]{0:T(128)S(1)} %copy-done.4, s32[512]{0:T(512)S(1)} %fusion.9), kind=kOutput, calls=%fused_computation.1 | convolution fusion | flops 100794368 | bytes 330240 | tf_op jit(solution)/shard_map/dot_general | solution.py:335
  50.2 12.6 %exchange.1 = f32[32,128]{1,0:T(8,128)} custom-call(f32[16,32,128]{2,1,0:T(8,128)} %bitcast.18), custom_call_target="tpu_custom_call" | custom-call | tf_op jit(solution)/shard_map/exchange/pallas_call | solution.py:339
  62.8 0.7 %slice_bitcast_fusion = f32[16,32]{0,1:T(8,128)S(1)} fusion(f32[32,128]{1,0:T(8,128)} %exchange.1), kind=kLoop, calls=%fused_computation.7 | loop fusion | bytes 4096 | tf_op jit(solution)/shard_map/transpose | solution.py:352
  63.6 0.7 %copy.17 = f32[16,32]{1,0:T(8,128)} copy(f32[16,32]{0,1:T(8,128)S(1)} %slice_bitcast_fusion) | data formatting | bytes 4096 | tf_op jit(solution)/shard_map/transpose | solution.py:352
  (1 shorter events, 0.0 us)
Async XLA Ops:
  11.8 5.6 %copy-start.1 = (f32[8,128]{1,0:T(8,128)S(1)}, f32[8,128]{1,0:T(8,128)}, u32[]{:S(2)}) copy-start(f32[8,128]{1,0:T(8,128)} %constant.70.clone.consts_ref) | copy-start | bytes 12292
  11.8 5.6 %copy-start.2 = (s32[16]{0:T(128)S(1)}, s32[16]{0:T(128)}, u32[]{:S(2)}) copy-start(s32[16]{0:T(128)} %depths_ref.1) | copy-start | bytes 196
  11.8 5.6 %copy-start.3 = (f32[16]{0:T(128)S(1)}, f32[16]{0:T(128)}, u32[]{:S(2)}) copy-start(f32[16]{0:T(128)} %ranges_ref.1) | copy-start | bytes 196
  17.4 1.2 %copy-start = (bf16[128,4096]{1,0:T(8,128)(2,1)S(1)}, bf16[128,4096]{1,0:T(8,128)(2,1)}, u32[]{:S(2)}) copy-start(bf16[128,4096]{1,0:T(8,128)(2,1)} %recorded_ref.1) | copy-start | bytes 3145732
  18.6 30.6 %copy-start.4 = (s32[128]{0:T(128)S(1)}, s32[128]{0:T(128)}, u32[]{:S(2)}) copy-start(s32[128]{0:T(128)} %param.15) | copy-start | bytes 1540

commit v2 on v1

--- a/solution.py
+++ b/solution.py
@@ -51,19 +51,6 @@
     return n // 2 if n % 2 == 0 else TERMS // 2 + n // 2
 
 
-def tile_groups(bins, modes, per_group):
-    runs = []
-    for group in range(bins // per_group):
-        last = (group + 1) * per_group - 1
-        top = min(modes, MMIN + (modes - MMIN) * last // max(bins - 1, 1) + SPREAD)
-        tiles = -(-top // LANES)
-        if runs and runs[-1][2] == tiles:
-            runs[-1][1] = group + 1
-        else:
-            runs.append([group, group + 1, tiles])
-    return runs
-
-
 def replica_kernel(
     shape,
     depths_ref,
@@ -71,11 +58,13 @@
     ranges_ref,
     consts_ref,
     wave_ref,
-    ampl_ref,
+    factor_ref,
+    source_ref,
     recorded_ref,
     out_ref,
-    re_ref,
-    im_ref,
+    sum_ref,
+    weight_ref,
+    term_ref,
     tab_ref,
     part_ref,
     psi_ref,
@@ -88,49 +77,55 @@
     first_x = place_ref[0]
     centre = place_ref[1]
 
-    def modal(start, tiles):
-        rows = pl.ds(pl.multiple_of(start, 8), 8)
-        cols = pl.ds(0, tiles * LANES)
-        wave = wave_ref[rows, cols]
-        cosine, sine = sincos_turns(wave * (centre * (1.0 / TWO_PI)))
-        xi = (wave - K_MID) * (1.0 / K_HALF)
-        twice = xi + xi
-        parts = []
-        for z in range(depth_grid):
-            ampl = ampl_ref[z, rows, cols]
-            parts.append((ampl * cosine, ampl * sine))
-        lane = lax.broadcasted_iota(jnp.int32, (8, LANES), 1)
-        total = jnp.zeros((8, LANES), jnp.float32)
-        before, now = None, None
+    for first in range(0, bins, LANES):
+        last = first + LANES - 1
+        top = min(modes, MMIN + (modes - MMIN) * last // max(bins - 1, 1) + SPREAD)
+        cols = slice(first, first + LANES)
+
+        def modal(step, sums, cols=cols):
+            start = pl.multiple_of(step * 8, 8)
+            rows = pl.ds(start, 8)
+            wave = wave_ref[rows, cols]
+            cosine, sine = sincos_turns(wave * (centre * (1.0 / TWO_PI)))
+            factor = factor_ref[rows, cols]
+            weight_ref[0:8, :] = factor * cosine
+            weight_ref[8:16, :] = factor * sine
+            xi = (wave - K_MID) * (1.0 / K_HALF)
+            before, now = jnp.ones_like(xi), xi
+            for n in range(1, TERMS):
+                term_ref[n * 8 : n * 8 + 8, :] = now
+                before, now = now, 2.0 * xi * now - before
+            sums = list(sums)
+            for i in range(8):
+                source = source_ref[jnp.minimum(start + i, modes - 1), :, cols].astype(jnp.float32)
+                value = jnp.concatenate(
+                    [source * weight_ref[i : i + 1, :], source * weight_ref[8 + i : 9 + i, :]], axis=0
+                )
+                sums[0] = sums[0] + value
+                for n in range(1, TERMS):
+                    sums[n] = sums[n] + value * term_ref[n * 8 + i : n * 8 + i + 1, :]
+            return tuple(sums)
+
+        zero = jnp.zeros((2 * depth_grid, LANES), jnp.float32)
+        sums = lax.fori_loop(0, -(-top // 8), modal, (zero,) * TERMS)
         for n in range(TERMS):
-            if n == 1:
-                before, now = jnp.ones_like(xi), xi
-            elif n > 1:
-                before, now = now, twice * now - before
             for z in range(depth_grid):
                 for c in range(2):
-                    product = parts[z][c] if n == 0 else parts[z][c] * now
-                    folded = product[:, :LANES]
-                    for tile in range(1, tiles):
-                        folded = folded + product[:, tile * LANES : (tile + 1) * LANES]
-                    value = jnp.sum(folded, axis=1, keepdims=True)
                     at = z * 2 * TERMS + c * TERMS + place_of(n)
-                    total = jnp.where(lane == at, value, total)
-        real_lane = lane % (2 * TERMS) < TERMS
-        swapped = jnp.where(
-            real_lane, pltpu.roll(total, LANES - TERMS, 1), -pltpu.roll(total, TERMS, 1)
-        )
-        re_ref[rows, :] = total
-        im_ref[rows, :] = swapped
-
-    for first, last, tiles in tile_groups(bins, modes, 32):
-
-        def body(i, carry, first=first, last=last, tiles=tiles):
-            count = last - first
-            modal((i // count) * quarter + (first + i % count) * 8, tiles)
-            return carry
-
-        lax.fori_loop(0, 4 * (last - first), body, 0)
+                    row = c * depth_grid + z
+                    sum_ref[at : at + 1, cols] = sums[n][row : row + 1, :]
+
+    def times_i(value):
+        blocks = []
+        for z in range(depth_grid):
+            base = z * 2 * TERMS
+            blocks.append(-value[base + TERMS : base + 2 * TERMS])
+            blocks.append(value[base : base + TERMS])
+        return jnp.concatenate(blocks, axis=0)
+
+    moments = sum_ref[...]
+    moments = jnp.concatenate([moments, -times_i(moments)], axis=0).astype(jnp.bfloat16)
+    group = depth_grid * 2 * TERMS
 
     for r in range(4):
         row = lax.broadcasted_iota(jnp.int32, (quarter, LANES), 0)
@@ -145,19 +140,14 @@
             tab_ref[:quarter, cols] = cosine.astype(jnp.bfloat16)
             tab_ref[quarter:, cols] = (-sine).astype(jnp.bfloat16)
             cosine, sine = cosine * step_c - sine * step_s, cosine * step_s + sine * step_c
-        rows = slice(r * quarter, (r + 1) * quarter)
-        left = jnp.concatenate([re_ref[rows, :].T, im_ref[rows, :].T], axis=1)
+        bin_row = lax.broadcasted_iota(jnp.int32, (bins, quarter), 0)
+        bin_column = lax.broadcasted_iota(jnp.int32, (bins, quarter), 1)
+        chosen = (bin_row == 4 * bin_column + r).astype(jnp.float32).astype(jnp.bfloat16)
+        picked = jnp.dot(moments, chosen, preferred_element_type=jnp.float32)
+        left = jnp.concatenate([picked[:group], picked[group:]], axis=1)
         part_ref[r] = jnp.dot(
             left.astype(jnp.bfloat16), tab_ref[...], preferred_element_type=jnp.float32
         )
-
-    def times_i(value):
-        blocks = []
-        for z in range(depth_grid):
-            base = z * 2 * TERMS
-            blocks.append(-value[base + TERMS : base + 2 * TERMS])
-            blocks.append(value[base : base + TERMS])
-        return jnp.concatenate(blocks, axis=0)
 
     for block in range(span // LANES):
         cols = slice(block * LANES, (block + 1) * LANES)
@@ -278,7 +268,6 @@
     sources = source_depths.shape[0]
     channels, samples = recorded.shape
     receivers = channels * count
-    width = -(-modes // LANES) * LANES
 
     first_x = 1.0 + 2.0 * (me * channels).astype(jnp.float32) / receivers
     reach = 2.0 * (channels - 1) / receivers
@@ -287,31 +276,27 @@
     assert 2.0 * (0.5 * top_phase) ** TERMS / math.factorial(TERMS) < 1e-9
     assert depth_grid * 2 * TERMS <= LANES
 
-    def regroup(value, fill):
-        value = jnp.pad(value, [(0, 0)] * (value.ndim - 1) + [(0, width - modes)], constant_values=fill)
-        shape = value.shape
-        value = value.reshape(shape[:-2] + (bins // 4, 4, width))
-        return jnp.swapaxes(value, -3, -2).reshape(shape)
-
-    wave = wavenumbers
-    live = jnp.arange(modes, dtype=jnp.int32)[None, :] < mode_counts[:, None]
-    factor = receiver_shapes.astype(jnp.float32) * (8.0 / math.sqrt(bins))
+    extra = -modes % 8
+    wave = wavenumbers.T
+    live = jnp.arange(modes, dtype=jnp.int32)[:, None] < mode_counts[None, :]
+    factor = receiver_shapes.T.astype(jnp.float32) * (8.0 / math.sqrt(bins))
     factor = jnp.where(live, factor / jnp.sqrt(wave * modes), 0.0)
-    ampl = jnp.swapaxes(source_shapes, 0, 1).astype(jnp.float32) * factor[None]
-    ampl = jnp.pad(ampl, ((0, LANES // (2 * TERMS) - depth_grid), (0, 0), (0, 0)))
-    shape = (bins, modes, LANES // (2 * TERMS), sources, channels, samples, receivers)
+    factor = jnp.pad(factor, ((0, extra), (0, 0)))
+    wave = jnp.pad(wave, ((0, extra), (0, 0)), constant_values=K_MID)
+    shape = (bins, modes, depth_grid, sources, channels, samples, receivers)
     matched = pl.pallas_call(
         functools.partial(replica_kernel, shape),
         out_shape=jax.ShapeDtypeStruct((channels, LANES), jnp.float32),
         in_specs=[pl.BlockSpec(memory_space=pltpu.SMEM)] * 3
-        + [pl.BlockSpec(memory_space=pltpu.VMEM)] * 4,
+        + [pl.BlockSpec(memory_space=pltpu.VMEM)] * 5,
         out_specs=pl.BlockSpec(memory_space=pltpu.VMEM),
         scratch_shapes=[
-            pltpu.VMEM((bins, LANES), jnp.float32),
-            pltpu.VMEM((bins, LANES), jnp.float32),
+            pltpu.VMEM((depth_grid * 2 * TERMS, bins), jnp.float32),
+            pltpu.VMEM((16, LANES), jnp.float32),
+            pltpu.VMEM((TERMS * 8, LANES), jnp.float32),
             pltpu.VMEM((bins // 2, samples // 4), jnp.bfloat16),
-            pltpu.VMEM((4, LANES, samples // 4), jnp.float32),
-            pltpu.VMEM((LANES, samples), jnp.bfloat16),
+            pltpu.VMEM((4, depth_grid * 2 * TERMS, samples // 4), jnp.float32),
+            pltpu.VMEM((depth_grid * 2 * TERMS, samples), jnp.bfloat16),
             pltpu.VMEM((sources, channels, 2 * TERMS), jnp.bfloat16),
         ],
         compiler_params=pltpu.CompilerParams(vmem_limit_bytes=48 * 1024 * 1024),
@@ -321,8 +306,9 @@
         jnp.stack([first_x, centre]),
         source_ranges,
         jnp.asarray(term_constants()),
-        regroup(wave, K_MID),
-        regroup(ampl, 0.0),
+        wave,
+        factor,
+        source_shapes.transpose(2, 1, 0),
         recorded,
     )
 

time: 64.7 us -> 38.6 us (0.60)
  local copies, waits for them, and re-layouts: 15.2 us -> 2.94 us
  Pallas kernels: 43.2 us -> 32.8 us
  other arithmetic: 4.76 us -> 1.48 us
    pallas_call x1, Pallas kernels: 30.6 us -> 20.2 us  [per_device(): pl.pallas_call(functools.partial(replica_kernel, shape), out_shape=jax.Sh...]
    unnamed x12 -> x14, local copies, waits for them, and re-layouts: 6.68 us -> 1.46 us
    mul x1 -> x0, other arithmetic: 3.36 us -> none  [per_device(): ampl = jnp.swapaxes(source_shapes, 0, 1).astype(jnp.float32) * factor[None]]
    pad x2, local copies, waits for them, and re-layouts: 2.66 us -> 0.09 us  [the longest x1 0.04 us: per_device(): factor = jnp.pad(factor, ((0, extra), (0, 0)))]
    reshape x1 -> x0, local copies, waits for them, and re-layouts: 2.26 us -> none  [regroup(): value = value.reshape(shape[:-2] + (bins // 4, 4, width))]
    transpose x2 -> x0, local copies, waits for them, and re-layouts: 2.2 us -> none  [regroup(): return jnp.swapaxes(value, -3, -2).reshape(shape)]
where the time goes in v2:
time: 38.6 us; the launch traced here: 38.4 us
  Pallas kernels  32.8 us (85%)
  local copies, waits for them, and re-layouts  2.94 us (8%)
  other arithmetic  1.48 us (4%)
  matrix products  1.03 us (3%)
    pallas_call x1, Pallas kernels, per_device(): pl.pallas_call(functools.partial(replica_kernel, shape), out_shape=jax.Sh...  20.2 us
    pallas_call x1, Pallas kernels, per_device(): pl.pallas_call(functools.partial(exchange_kernel, (freq_size, sub_size)),...  12.6 us
    unnamed x14, local copies, waits for them, and re-layouts  1.46 us
    select_n x1, other arithmetic, per_device(): factor = jnp.where(live, factor / jnp.sqrt(wave * modes), 0.0)  1.4 us
    transpose x2, local copies, waits for them, and re-layouts, per_device(): return total[:own, :sources].T  1.39 us
    dot_general x1, matrix products, per_device(): jnp.dot(member, matched, precision=lax.Precision.HIGHEST)  1.03 us

profile of v2, /device:TPU:0, one launch (start us, length us, event | category | flops | bytes accessed | tf_op | source)
XLA Modules:
  0.0 38.4 jit_solution(1303917423181780019)
XLA Ops:
  0.0 0.1 pad_maximum_fusion.place_ref
  0.1 0.0 copy-start.5
  0.1 1.4 %fusion = f32[300,512]{1,0:T(8,128)S(1)} fusion(bf16[512,300]{0,1:T(8,128)(2,1)} %param.10, s32[512]{0:T(512)} %param.12, f32[512,300]{0,1:T(8,128)} %param.9), kind=kLoop, calls=%fused_computation.2 | loop fusion | flops 921600 | bytes 1538048 | tf_op jit(solution)/shard_map/jit(_where)/select_n | solution.py:283
  1.5 0.0 copy-start
  1.5 0.0 copy-start.1
  1.5 0.0 copy-start.2
  1.5 0.0 copy-start.3
  1.5 0.0 copy-start.4
  1.6 0.0 copy-done.5
  1.7 1.1 %copy-done = bf16[512,4,300]{0,1,2:T(4,128)(2,1)S(1)} copy-done((bf16[512,4,300]{0,1,2:T(4,128)(2,1)S(1)}, bf16[512,4,300]{0,1,2:T(4,128)(2,1)}, u32[]{:S(2)}) %copy-start) | copy-done | bytes 1228824
  2.8 0.3 copy-done.1
  3.1 0.0 copy-done.2
  3.1 0.0 copy-done.3
  3.1 0.0 copy-done.4
  3.1 0.0 copy-start.6
  3.1 20.2 %replica.1 = f32[128,128]{1,0:T(8,128)S(1)} custom-call(s32[16]{0:T(128)S(1)} %copy-done.3, f32[2]{0:T(128)S(1)} %pad_maximum_fusion.place_ref, f32[16]{0:T(128)S(1)} %copy-done.4, f32[8,128]{1,0:T(8,128)S(1)} %copy-done.2, f32[304,512]{1,0:T(8,128)S(1)} %pad.8.wave_ref, f32[304,512]{1,0:T(8,128)S(1)} %pad.9.factor_ref, bf16[300,4,512]{2,1,0:T(4,128)(2,1)S(1)} %bitcast.13, ...), custom_call_target="tpu_custom_call" | custom-call | tf_op jit(solution)/shard_map/replica/pallas_call | solution.py:287
  23.3 0.0 copy-done.6
  23.4 1.0 %convolution_multiply_fusion = f32[512,128]{1,0:T(8,128)} fusion(f32[128,128]{1,0:T(8,128)S(1)} %replica.1, s32[128]{0:T(128)S(1)} %copy-done.6, s32[512]{0:T(512)S(1)} %fusion.10), kind=kOutput, calls=%fused_computation | convolution fusion | flops 100794368 | bytes 330240 | tf_op jit(solution)/shard_map/dot_general | solution.py:321
  24.4 12.6 %exchange.1 = f32[32,128]{1,0:T(8,128)} custom-call(f32[16,32,128]{2,1,0:T(8,128)} %bitcast.15), custom_call_target="tpu_custom_call" | custom-call | tf_op jit(solution)/shard_map/exchange/pallas_call | solution.py:325
  37.0 0.7 %slice_bitcast_fusion = f32[16,32]{0,1:T(8,128)S(1)} fusion(f32[32,128]{1,0:T(8,128)} %exchange.1), kind=kLoop, calls=%fused_computation.7 | loop fusion | bytes 4096 | tf_op jit(solution)/shard_map/transpose | solution.py:338
  37.7 0.7 %copy.10 = f32[16,32]{1,0:T(8,128)} copy(f32[16,32]{0,1:T(8,128)S(1)} %slice_bitcast_fusion) | data formatting | bytes 4096 | tf_op jit(solution)/shard_map/transpose | solution.py:338
  (3 shorter events, 0.1 us)
Async XLA Ops:
  0.1 1.5 %copy-start.5 = (f32[512,300]{0,1:T(8,128)S(1)}, f32[512,300]{0,1:T(8,128)}, u32[]{:S(2)}) copy-start(f32[512,300]{0,1:T(8,128)} %param.9) | copy-start | bytes 1843204
  1.5 1.3 %copy-start = (bf16[512,4,300]{0,1,2:T(4,128)(2,1)S(1)}, bf16[512,4,300]{0,1,2:T(4,128)(2,1)}, u32[]{:S(2)}) copy-start(bf16[512,4,300]{0,1,2:T(4,128)(2,1)} %param.11) | copy-start | bytes 3686404
  1.5 1.6 %copy-start.1 = (bf16[128,4096]{1,0:T(8,128)(2,1)S(1)}, bf16[128,4096]{1,0:T(8,128)(2,1)}, u32[]{:S(2)}) copy-start(bf16[128,4096]{1,0:T(8,128)(2,1)} %recorded_ref.1) | copy-start | bytes 3145732
  1.5 1.6 %copy-start.2 = (f32[8,128]{1,0:T(8,128)S(1)}, f32[8,128]{1,0:T(8,128)}, u32[]{:S(2)}) copy-start(f32[8,128]{1,0:T(8,128)} %constant.71.clone.consts_ref) | copy-start | bytes 12292
  1.5 1.6 %copy-start.3 = (s32[16]{0:T(128)S(1)}, s32[16]{0:T(128)}, u32[]{:S(2)}) copy-start(s32[16]{0:T(128)} %depths_ref.1) | copy-start | bytes 196
  1.5 1.6 %copy-start.4 = (f32[16]{0:T(128)S(1)}, f32[16]{0:T(128)}, u32[]{:S(2)}) copy-start(f32[16]{0:T(128)} %ranges_ref.1) | copy-start | bytes 196
  3.1 20.3 %copy-start.6 = (s32[128]{0:T(128)S(1)}, s32[128]{0:T(128)}, u32[]{:S(2)}) copy-start(s32[128]{0:T(128)} %param.15) | copy-start | bytes 1540

commit v3 on v2

--- a/solution.py
+++ b/solution.py
@@ -191,7 +191,7 @@
                 total = total + product[:, tile * LANES : (tile + 1) * LANES]
         value = jnp.sum(total, axis=1, keepdims=True)
         lane = lax.broadcasted_iota(jnp.int32, (channels, LANES), 1)
-        return jnp.where(lane == s, value, matched)
+        return jnp.where(lane % sources == s, value, matched)
 
     out_ref[...] = lax.fori_loop(
         0, sources, source, jnp.zeros((channels, LANES), jnp.float32)
@@ -314,11 +314,18 @@
 
     section_count = receivers // 4
     own = section_count // count
-    padded = -(-own // 8) * 8
+    per_row = min(LANES // sources, own)
+    own_rows = own // per_row
+    assert LANES % sources == 0 and own % per_row == 0
+    padded = -(-own_rows // 8) * 8
     slot = jnp.arange(count * padded, dtype=jnp.int32)
-    wanted = jnp.where(slot % padded < own, slot // padded * own + slot % padded, -1)
-    member = (wanted[:, None] == sections[None, :]).astype(jnp.float32)
-    blocks = jnp.dot(member, matched, precision=lax.Precision.HIGHEST) * (
+    wanted = jnp.where(
+        slot % padded < own_rows, slot // padded * own_rows + slot % padded, -1
+    )
+    member = (wanted[:, None] == (sections // per_row)[None, :]).astype(jnp.float32)
+    lane_part = jnp.arange(LANES, dtype=jnp.int32) // sources
+    kept = jnp.where((sections % per_row)[:, None] == lane_part[None, :], matched, 0.0)
+    blocks = jnp.dot(member, kept, precision=lax.Precision.HIGHEST) * (
         1.0 / math.sqrt(samples * (receivers // section_count))
     )
     blocks = blocks.reshape(count, padded, LANES)
@@ -335,7 +342,8 @@
         compiler_params=pltpu.CompilerParams(collective_id=0, has_side_effects=True),
         name="exchange",
     )(blocks)
-    return total[:own, :sources].T
+    total = total[:own_rows, : per_row * sources].reshape(own_rows, per_row, sources)
+    return total.transpose(2, 0, 1).reshape(sources, own)
 
 
 def solution(mesh):

time: 38.6 us -> 36.4 us (0.943)
  Pallas kernels: 32.8 us -> 30.7 us
    pallas_call x1, Pallas kernels: 12.6 us -> 10.5 us  [per_device(): pl.pallas_call(functools.partial(exchange_kernel, (freq_size, sub_size)),...]
    transpose x2 -> x0, local copies, waits for them, and re-layouts: 1.39 us -> none  [per_device(): return total[:own, :sources].T]
    reshape x0 -> x2, local copies, waits for them, and re-layouts: none -> 0.76 us  [the longest x1 0.68 us: per_device(): return total.transpose(2, 0, 1).reshape(sources, own)]
    slice x0 -> x1, local copies, waits for them, and re-layouts: none -> 0.68 us  [per_device(): total[:own_rows, :per_row * sources].reshape(own_rows, per_row, sources)]
where the time goes in v3:
time: 36.4 us; the launch traced here: 36.2 us
  Pallas kernels  30.7 us (84%)
  local copies, waits for them, and re-layouts  2.98 us (8%)
  other arithmetic  1.49 us (4%)
  matrix products  0.87 us (2%)
    pallas_call x1, Pallas kernels, per_device(): pl.pallas_call(functools.partial(replica_kernel, shape), out_shape=jax.Sh...  20.2 us
    pallas_call x1, Pallas kernels, per_device(): pl.pallas_call(functools.partial(exchange_kernel, (freq_size, sub_size)),...  10.5 us
    unnamed x14, local copies, waits for them, and re-layouts  1.46 us
    select_n x1, other arithmetic, per_device(): factor = jnp.where(live, factor / jnp.sqrt(wave * modes), 0.0)  1.4 us
    dot_general x1, matrix products, per_device(): jnp.dot(member, kept, precision=lax.Precision.HIGHEST)  0.87 us

profile of v3, /device:TPU:0, one launch (start us, length us, event | category | flops | bytes accessed | tf_op | source)
XLA Modules:
  0.0 36.2 jit_solution(5825967936083993040)
XLA Ops:
  0.0 0.1 pad_maximum_fusion.place_ref
  0.1 0.0 copy-start.5
  0.1 1.4 %fusion.1 = f32[300,512]{1,0:T(8,128)S(1)} fusion(bf16[512,300]{0,1:T(8,128)(2,1)} %param.10, s32[512]{0:T(512)} %param.12, f32[512,300]{0,1:T(8,128)} %param.9), kind=kLoop, calls=%fused_computation.3 | loop fusion | flops 921600 | bytes 1538048 | tf_op jit(solution)/shard_map/jit(_where)/select_n | solution.py:283
  1.5 0.0 copy-start
  1.5 0.0 copy-start.1
  1.5 0.0 copy-start.2
  1.5 0.0 copy-start.3
  1.5 0.0 copy-start.4
  1.6 0.0 copy-done.5
  1.7 1.1 %copy-done = bf16[512,4,300]{0,1,2:T(4,128)(2,1)S(1)} copy-done((bf16[512,4,300]{0,1,2:T(4,128)(2,1)S(1)}, bf16[512,4,300]{0,1,2:T(4,128)(2,1)}, u32[]{:S(2)}) %copy-start) | copy-done | bytes 1228824
  2.8 0.3 copy-done.1
  3.1 0.0 copy-done.2
  3.1 0.0 copy-done.3
  3.1 0.0 copy-done.4
  3.1 0.0 copy-start.6
  3.1 20.2 %replica.1 = f32[128,128]{1,0:T(8,128)S(1)} custom-call(s32[16]{0:T(128)S(1)} %copy-done.3, f32[2]{0:T(128)S(1)} %pad_maximum_fusion.place_ref, f32[16]{0:T(128)S(1)} %copy-done.4, f32[8,128]{1,0:T(8,128)S(1)} %copy-done.2, f32[304,512]{1,0:T(8,128)S(1)} %pad.8.wave_ref, f32[304,512]{1,0:T(8,128)S(1)} %pad.9.factor_ref, bf16[300,4,512]{2,1,0:T(4,128)(2,1)S(1)} %bitcast.14, ...), custom_call_target="tpu_custom_call" | custom-call | tf_op jit(solution)/shard_map/replica/pallas_call | solution.py:287
  23.3 0.0 copy-done.6
  23.4 0.9 %fusion.block_ref = f32[16,8,128]{2,1,0:T(8,128)} fusion(f32[128,128]{1,0:T(8,128)S(1)} %replica.1, s32[128]{0:T(128)S(1)} %get-tuple-element.7, s32[128]{0:T(128)S(1)} %get-tuple-element.6, s32[128]{0:T(128)S(1)} %get-tuple-element.5, s32[128]{0:T(128)S(1)} %compare_select_fusion), kind=kOutput, calls=%fused_computation.1 | convolution fusion | flops 25231360 | bytes 133120 | tf_op jit(solution)/shard_map/dot_general | solution.py:328
  24.2 10.5 %exchange.1 = f32[8,128]{1,0:T(8,128)} custom-call(f32[16,8,128]{2,1,0:T(8,128)} %fusion.block_ref), custom_call_target="tpu_custom_call" | custom-call | tf_op jit(solution)/shard_map/exchange/pallas_call | solution.py:332
  34.7 0.7 %slice.3 = f32[4,128]{1,0:T(4,128)S(1)} slice(f32[8,128]{1,0:T(8,128)} %exchange.1), slice={[0:4], [0:128]} | slice | bytes 4096 | tf_op jit(solution)/shard_map/slice | solution.py:345
  35.4 0.1 reshape.52
  35.5 0.7 %copy.11 = f32[16,32]{1,0:T(8,128)} copy(f32[16,32]{0,1:T(8,128)S(1)} %bitcast.16) | data formatting | bytes 4096 | tf_op jit(solution)/shard_map/reshape | solution.py:346
  (4 shorter events, 0.1 us)
Async XLA Ops:
  0.1 1.5 %copy-start.5 = (f32[512,300]{0,1:T(8,128)S(1)}, f32[512,300]{0,1:T(8,128)}, u32[]{:S(2)}) copy-start(f32[512,300]{0,1:T(8,128)} %param.9) | copy-start | bytes 1843204
  1.5 1.3 %copy-start = (bf16[512,4,300]{0,1,2:T(4,128)(2,1)S(1)}, bf16[512,4,300]{0,1,2:T(4,128)(2,1)}, u32[]{:S(2)}) copy-start(bf16[512,4,300]{0,1,2:T(4,128)(2,1)} %param.11) | copy-start | bytes 3686404
  1.5 1.6 %copy-start.1 = (bf16[128,4096]{1,0:T(8,128)(2,1)S(1)}, bf16[128,4096]{1,0:T(8,128)(2,1)}, u32[]{:S(2)}) copy-start(bf16[128,4096]{1,0:T(8,128)(2,1)} %recorded_ref.1) | copy-start | bytes 3145732
  1.5 1.6 %copy-start.2 = (f32[8,128]{1,0:T(8,128)S(1)}, f32[8,128]{1,0:T(8,128)}, u32[]{:S(2)}) copy-start(f32[8,128]{1,0:T(8,128)} %constant.95.clone.consts_ref) | copy-start | bytes 12292
  1.5 1.6 %copy-start.3 = (s32[16]{0:T(128)S(1)}, s32[16]{0:T(128)}, u32[]{:S(2)}) copy-start(s32[16]{0:T(128)} %depths_ref.1) | copy-start | bytes 196
  1.5 1.6 %copy-start.4 = (f32[16]{0:T(128)S(1)}, f32[16]{0:T(128)}, u32[]{:S(2)}) copy-start(f32[16]{0:T(128)} %ranges_ref.1) | copy-start | bytes 196
  3.1 20.2 %copy-start.6 = (s32[128]{0:T(128)S(1)}, s32[128]{0:T(128)}, u32[]{:S(2)}) copy-start(s32[128]{0:T(128)} %param.15) | copy-start | bytes 1540
